TPU v7x, 128 devices: a whole 4x4x4 slice. The times are simulated.
128 devices in a mesh: dp: 16 (over z_hi, y, core), ctx: 8 (over x, z_lo).
Axes of the slice: x: 4, y: 4, z: 4 (z_hi: 2, z_lo: 2; z = z_hi * 2 + z_lo), core: 2. Of those that a mesh axis runs over, the one named last changes fastest.
Arguments:
- hidden: bfloat16 [16, 3072, 8192], P('dp', 'ctx'), may hold values from -6 to 6
- queries: bfloat16 [16, 3072, 4096], P('dp', 'ctx'), may hold values from -136 to 136
- weights_old: float32 [8192, 1024], P(('dp', 'ctx')), may hold values from -0.0625 to 0.0625
- gradient_old: float32 [8192, 1024], P(('dp', 'ctx')), may hold values from -6 to 6
- first_old: float32 [8192, 1024], P(('dp', 'ctx')), may hold values from -4 to 4
- second_old: float32 [8192, 1024], P(('dp', 'ctx')), may hold values from 0.25 to 4
- old_owner: int32 [128], replicated, may hold values from 0 to 127, each once
- new_owner: int32 [128], replicated, may hold values from 0 to 127, each once
- offsets: int32 [16, 8, 2], P('dp'), may hold values from 0 to 2880, as said below
Outputs:
- weights_new: float32 [1024, 8192], P(('dp', 'ctx'))
- first_new: float32 [1024, 8192], P(('dp', 'ctx'))
- second_new: float32 [1024, 8192], P(('dp', 'ctx'))
- attended: bfloat16 [16, 3072, 4096], P('dp', 'ctx')
Inputs may be any that keep to these rules, and one draw needn't show every extreme that they name: `offsets`: for sequence b and ctx index c the two entries are p * 192 and (15 - p) * 192, where p runs over a permutation of the ctx indices drawn for each sequence. `old_owner`: each block index appears once. `new_owner`: each block index appears once.
All inputs are finite; a program needn't handle non-finite values.
Results may differ from a plain program's by a relative error of at most 0.0055.
The roundings to bfloat16 on the way count: a program that leaves them out, or rounds other values in their place, can miss the bound.
Values may be sent and summed in bfloat16 or wider, within the bound.
No kernel may reach another device: no remote copies, remote signals or barrier semaphores. Data moves between devices by JAX's collectives and lax.ppermute only.
A program may use at most 320 MiB of HBM per device.

v0:
```python
import math
import jax
import jax.numpy as jnp
from jax import lax
from jax.sharding import PartitionSpec as P

HEAD = 128
KV_HEADS = 4
Q_HEADS = 32
learn_rate = 0.0003
beta_one = 0.9
beta_two = 0.95
adam_eps = 1e-08
decay_rate = 0.1
step_number = 1000
corr_one = 1.0 - beta_one**step_number
corr_two = 1.0 - beta_two**step_number
rope_base = 500000.0


def in_blocks(value, dim, peers):
    before, after = (value.shape[:dim], value.shape[dim + 1 :])
    return jnp.moveaxis(value.reshape(*before, peers, -1, *after), dim, 0)


def joined_along(tiles, dim):
    dims = list(tiles.shape[1:])
    dims[dim] *= tiles.shape[0]
    return jnp.moveaxis(tiles, 0, dim).reshape(dims)


def one_exchange(value, axis, axes, splits, concats):
    sizes = [lax.axis_size(a) for a in axes]
    tiles = in_blocks(value, splits[0], sizes[0])
    tiles = jnp.moveaxis(in_blocks(tiles, splits[1] + 1, sizes[1]), 0, 1)
    inside = tiles.shape[2:]
    tiles = tiles.reshape(-1, *inside)
    tiles = lax.all_to_all(tiles, axis, split_axis=0, concat_axis=0, tiled=True)
    tiles = joined_along(tiles.reshape(*sizes, *inside), concats[0] + 1)
    return joined_along(tiles, concats[1])


def adam_step(weights, gradient, first_mom, second_mom):
    first_next = beta_one * first_mom + (1.0 - beta_one) * gradient
    second_next = beta_two * second_mom + (1.0 - beta_two) * gradient * gradient
    direction = first_next / corr_one / (jnp.sqrt(second_next / corr_two) + adam_eps)
    weights_next = weights - learn_rate * (direction + decay_rate * weights)
    return (weights_next, first_next, second_next)


def rotate_keys(key_heads, positions):
    head_dim = key_heads.shape[-1]
    half_dim = head_dim // 2
    exponent = jnp.arange(half_dim, dtype=jnp.float32) * (2.0 / head_dim)
    inv_freq = jnp.power(rope_base, -exponent)
    angles = positions.astype(jnp.float32)[..., None] * inv_freq
    cosine = jnp.cos(angles)[..., None, :]
    sine_part = jnp.sin(angles)[..., None, :]
    first_half = key_heads[..., :half_dim]
    second_half = key_heads[..., half_dim:]
    return jnp.concatenate(
        [
            first_half * cosine - second_half * sine_part,
            second_half * cosine + first_half * sine_part,
        ],
        axis=-1,
    )


def invert(owners):
    devices = owners.shape[0]
    return jnp.zeros((devices,), jnp.int32).at[owners].set(jnp.arange(devices, dtype=jnp.int32))


def relocate(stacked, new_owner, old_owner):
    states_count, row_count, proj_width = stacked.shape
    devices = new_owner.shape[0]
    col_count = proj_width // devices
    outgoing = stacked.reshape(states_count, row_count, devices, col_count).transpose(2, 0, 3, 1)
    outgoing = jnp.take(outgoing, new_owner, axis=0)
    grid_form = outgoing.reshape((lax.axis_size("dp"), lax.axis_size("ctx")) + outgoing.shape[1:])
    incoming = one_exchange(grid_form, ("dp", "ctx"), ("dp", "ctx"), (0, 1), (0, 1)).reshape(
        outgoing.shape
    )
    ordered = jnp.take(incoming, invert(old_owner), axis=0)
    return ordered.transpose(1, 2, 0, 3).reshape(states_count, col_count, devices * row_count)


def shards(
    hidden, queries, weights_old, gradient_old, first_old, second_old, old_owner, new_owner, offsets
):
    devices = old_owner.shape[0]
    row_count, proj_width = weights_old.shape
    tok_rows = hidden.shape[1]
    half_tok = tok_rows // 2
    model_width = hidden.shape[2]
    head_dim = HEAD
    kv_heads = KV_HEADS
    groups = Q_HEADS // KV_HEADS
    key_width = kv_heads * head_dim
    tokens_flat = hidden[0]
    updated = adam_step(weights_old, gradient_old, first_old, second_old)
    moved = relocate(jnp.stack(updated), new_owner, old_owner)
    weights_new, first_new, second_new = (moved[0], moved[1], moved[2])
    weights_next = adam_step(weights_old, gradient_old, first_old, second_old)[0]
    copies = weights_next.astype(jnp.bfloat16)
    permuted = jnp.take(
        tokens_flat.reshape(tok_rows, devices, row_count), old_owner, axis=1
    ).reshape(tok_rows, model_width)
    segment = lax.all_gather(copies, ("dp", "ctx"), axis=0, tiled=True)
    columns = lax.slice_in_dim(permuted, 0, segment.shape[0], axis=1)
    projected = jnp.zeros((tok_rows, proj_width), jnp.float32) + jnp.dot(
        columns, segment, preferred_element_type=jnp.float32
    )
    offset_table = offsets[0]
    ctx_count = offset_table.shape[0]
    flat_table = offset_table.reshape(2 * ctx_count)
    slot_ids = jnp.arange(2 * ctx_count, dtype=jnp.int32)

    def lookup(rows_global):
        device_of = rows_global // tok_rows
        local_row = rows_global % tok_rows
        slot_index = device_of * 2 + local_row // half_tok
        picked = slot_index[:, None] == slot_ids[None, :]
        return jnp.sum(jnp.where(picked, flat_table[None, :], 0), axis=1) + local_row % half_tok

    own_rows = lax.axis_index("ctx") * tok_rows + jnp.arange(tok_rows, dtype=jnp.int32)
    query_pos = lookup(own_rows)
    key_heads = projected[:, :key_width].reshape(tok_rows, kv_heads, head_dim)
    key_rows = rotate_keys(key_heads, query_pos).reshape(tok_rows, key_width).astype(jnp.bfloat16)
    value_rows = projected[:, key_width:].astype(jnp.bfloat16)
    query_heads = queries[0].reshape(tok_rows, kv_heads, groups, head_dim)
    inv_root = 1.0 / math.sqrt(head_dim)
    best_score = jnp.full((kv_heads, groups, tok_rows), -1e30, jnp.float32)
    key_block = lax.all_gather(key_rows, "ctx", axis=0, tiled=True)
    value_block = lax.all_gather(value_rows, "ctx", axis=0, tiled=True)
    block_rows = key_block.shape[0]
    key_pos = lookup(jnp.arange(block_rows, dtype=jnp.int32))
    key_split = key_block.reshape(block_rows, kv_heads, head_dim)
    scores = (
        jnp.einsum("tkgd,nkd->kgtn", query_heads, key_split, preferred_element_type=jnp.float32)
        * inv_root
    )
    visible = key_pos[None, None, None, :] <= query_pos[None, None, :, None]
    masked = jnp.where(visible, scores, -1e30)
    best_next = jnp.maximum(best_score, jnp.max(masked, axis=3))
    exp_terms = jnp.where(visible, jnp.exp(masked - best_next[..., None]), 0.0)
    totals_next = jnp.sum(exp_terms, axis=3)
    value_split = value_block.reshape(block_rows, kv_heads, head_dim)
    increment = jnp.einsum(
        "kgtn,nkd->tkgd",
        exp_terms.astype(jnp.bfloat16),
        value_split,
        preferred_element_type=jnp.float32,
    )
    result = increment / jnp.transpose(totals_next, (2, 0, 1))[..., None]
    attended = result.reshape(1, tok_rows, Q_HEADS * head_dim).astype(jnp.bfloat16)
    return (weights_new, first_new, second_new, attended)


def solution(mesh):
    in_specs = (
        P("dp", "ctx", None),
        P("dp", "ctx", None),
        P(("dp", "ctx"), None),
        P(("dp", "ctx"), None),
        P(("dp", "ctx"), None),
        P(("dp", "ctx"), None),
        P(),
        P(),
        P("dp", None, None),
    )
    out_specs = (
        P(("dp", "ctx"), None),
        P(("dp", "ctx"), None),
        P(("dp", "ctx"), None),
        P("dp", "ctx", None),
    )
    return jax.shard_map(shards, mesh=mesh, in_specs=in_specs, out_specs=out_specs, check_vma=False)
```

profile of v0, /device:TPU:4, one launch (start us, length us, event | category | flops | bytes accessed | tf_op | source)
XLA Modules:
  0.0 606.7 jit_solution(16304854576319501626)
XLA Ops:
  7.2 2.0 fusion.45
  9.3 0.8 copy.64
  10.2 8.6 %copy.63 = bf16[1,384,8192]{1,2,0:T(8,128)(2,1)} copy(bf16[1,384,8192]{2,1,0:T(8,128)(2,1)} %param.11) | data formatting | bytes 12582912 | tf_op args[0]
  18.8 0.1 broadcast_in_dim.86
  18.9 0.1 broadcast_in_dim.87
  19.0 6.8 %gather_fusion = bf16[128,384,64]{1,2,0:T(8,128)(2,1)} fusion(bf16[384,128,64]{0,2,1:T(8,128)(2,1)} %bitcast.75, s32[1024]{0:T(1024)S(1)} %pad_clamp_fusion), kind=kCustom, calls=%fused_computation.2 | custom fusion | bytes 12583424 | tf_op jit(solution)/shard_map/jit(_take)/gather | solution.py:107
  25.9 0.1 select_reduce_fusion.1
  26.0 0.8 multiply_cosine_fusion
  26.8 8.0 %bitcast_select_fusion.1 = bf16[384,8192]{0,1:T(8,128)(2,1)} fusion(bf16[128,384,64]{1,2,0:T(8,128)(2,1)} %gather_fusion, pred[8192]{0:T(1024)(128)(4,1)S(1)} %broadcast_in_dim.87), kind=kLoop, calls=%fused_computation.11 | loop fusion | flops 3145728 | bytes 12591104 | tf_op jit(solution)/shard_map/jit(_take)/select_n | solution.py:107
  34.8 299.3 %all-gather.4.cloned.1.call-done = bf16[8192,1024]{1,0:T(8,128)(2,1)} async-done(((bf16[64,1024]{1,0:T(8,128)(2,1)}), bf16[8192,1024]{1,0:T(8,128)(2,1)}) %all-gather.4.cloned.1.call-update) | async-done | bytes 16777232 | tf_op jit(solution)/shard_map/all_gather | solution.py:110
  334.1 12.2 %fusion.48 = f32[384,1024]{1,0:T(8,128)S(1)} fusion(bf16[384,8192]{0,1:T(8,128)(2,1)} %bitcast_select_fusion.1, bf16[8192,1024]{1,0:T(8,128)(2,1)} %all-gather.4.cloned.1.call-done), kind=kOutput, calls=%fused_computation.93 | convolution fusion | flops 6442450944 | bytes 24641536 | tf_op jit(solution)/shard_map/dot_general | solution.py:112
  346.3 1.2 copy-done
  347.5 0.3 reshape.259
  347.8 0.6 subtract_convert_fusion
  348.4 0.5 pad_maximum_fusion
  349.0 1.0 copy.65
  350.0 0.2 copy.55
  350.2 0.2 copy.54
  350.4 0.2 copy.53
  350.7 0.1 maximum_bitcast_fusion
  350.8 0.8 gather_fusion.1
  351.6 0.2 select_bitcast_fusion.1
  351.8 1.9 reshape.305
  353.7 9.9 %all-to-all-start = ((f32[128,1,1536]{2,1,0:T(1,128)}), f32[128,1,1536]{2,1,0:T(1,128)S(1)}, u32[]{:S(2)}, u32[]{:S(2)}) async-start(f32[128,1,1536]{2,1,0:T(1,128)} %reshape.305), calls=%async_computation | async-start | bytes 1572864 | tf_op jit(solution)/shard_map/all_to_all | solution.py:38
  363.6 4.4 copy.77
  368.0 1.0 scatter_custom_fusion
  369.0 0.1 select_reduce_fusion
  369.2 2.4 broadcast_compare_fusion
  371.6 7.1 %all-to-all-done = f32[128,1,1536]{2,1,0:T(1,128)S(1)} async-done(((f32[128,1,1536]{2,1,0:T(1,128)}), f32[128,1,1536]{2,1,0:T(1,128)S(1)}, u32[]{:S(2)}, u32[]{:S(2)}) %all-to-all-start) | async-done | bytes 786464 | tf_op jit(solution)/shard_map/all_to_all | solution.py:38
  378.8 0.5 broadcast.364
  379.3 2.5 reduce
  381.8 0.3 reshape.306
  382.1 0.8 gather_fusion.2
  382.9 0.2 select_bitcast_fusion
  383.1 0.1 fusion.47
  383.3 0.1 copy.60
  383.4 0.9 squeeze.9
  384.3 0.1 copy.61
  384.4 0.9 squeeze.10
  385.2 0.1 copy.62
  385.3 0.9 squeeze.11
  386.2 1.9 slice.50
  388.2 42.9 %all-gather.8.cloned.1.call-done = bf16[3072,512]{0,1:T(8,128)(2,1)} async-done(((bf16[384,512]{0,1:T(8,128)(2,1)}), bf16[3072,512]{0,1:T(8,128)(2,1)}) %all-gather.8.cloned.1.call-update) | async-done | bytes 3145744 | tf_op jit(solution)/shard_map/all_gather | solution.py:135
  431.1 56.4 %fusion = (f32[4,8,384]{2,1,0:T(8,128)S(1)}, f32[4,3072,384,8]{2,1,3,0:T(8,128)}) fusion(pred[384,3072]{0,1:T(8,128)(4,1)S(1)} %copy-done.1, bf16[3072,4,128,1]{0,2,3,1:T(8,128)(2,1)} %bitcast.86, bf16[384,4,8,128]{3,2,1,0:T(8,128)(2,1)} %bitcast.78), kind=kOutput, calls=%fused_computation.6 | convolution fusion | flops 9776910336 | bytes 158515200 | tf_op jit(solution)/shard_map/tkgd,nkd->kgtn/dot_general | solution.py:141
  487.5 46.2 %fusion.1 = f32[4,8,384]{2,1,0:T(8,128)S(1)} fusion(f32[4,3072,384,8]{2,1,3,0:T(8,128)} %get-tuple-element.35, f32[4,8,384]{2,1,0:T(8,128)S(1)} %broadcast_maximum_fusion, pred[384,3072]{0,1:T(8,128)(4,1)S(1)} %copy-done.1), kind=kLoop, calls=%fused_computation.7 | loop fusion | flops 188731392 | bytes 152272896 | tf_op jit(solution)/shard_map/reduce_sum | solution.py:148
  533.8 4.9 copy.74
  538.6 56.9 %fusion.6 = bf16[384,4,8,128]{0,3,2,1:T(8,128)(2,1)} fusion(f32[384,4,8]{0,2,1:T(8,128)S(1)} %bitcast.85, bf16[3072,4,128,1]{0,2,3,1:T(8,128)(2,1)} %bitcast.79, f32[4,3072,384,8]{2,1,3,0:T(8,128)} %get-tuple-element.35, f32[4,8,384]{2,1,0:T(8,128)S(1)} %broadcast_maximum_fusion, pred[384,3072]{0,1:T(8,128)(4,1)S(1)} %copy-done.1), kind=kOutput, calls=%fused_computation.13 | convolution fusion | flops 9855565824 | bytes 158564352 | tf_op jit(solution)/shard_map/kgtn,nkd->tkgd/dot_general | solution.py:150
  595.6 4.6 copy.70
  (32 shorter events, 0.5 us)
Async XLA Ops:
  7.2 326.9 %all-gather.4.cloned.1.call-start = ((), (), s32[]{:S(2)}) async-start(), calls=%async_computation.1 | async-start | bytes 16908288 | tf_op jit(solution)/shard_map/all_gather | solution.py:110
  9.3 421.8 %all-gather.8.cloned.1.call-start = ((), (), s32[]{:S(2)}) async-start(), calls=%async_computation.3 | async-start | bytes 3538944 | tf_op jit(solution)/shard_map/all_gather | solution.py:135
  10.2 8.6 %copy-start.2 = (s32[128]{0:T(128)S(1)}, s32[128]{0:T(128)}, u32[]{:S(2)}) copy-start(s32[128]{0:T(128)} %param.17) | copy-start | bytes 1540
  346.3 1.2 copy-start
  347.5 3.1 copy-start.3
  353.7 25.1 %all-to-all-start = ((f32[128,1,1536]{2,1,0:T(1,128)}), f32[128,1,1536]{2,1,0:T(1,128)S(1)}, u32[]{:S(2)}, u32[]{:S(2)}) async-start(f32[128,1,1536]{2,1,0:T(1,128)} %reshape.305), calls=%async_computation | async-start | bytes 1572864 | tf_op jit(solution)/shard_map/all_to_all | solution.py:38
  363.6 170.2 %all-gather.6.cloned.1.call-start = ((), (), s32[]{:S(2)}) async-start(), calls=%async_computation.2 | async-start | bytes 3538944 | tf_op jit(solution)/shard_map/all_gather | solution.py:136
  383.1 48.0 %copy-start.1 = (pred[384,3072]{0,1:T(8,128)(4,1)S(1)}, pred[384,3072]{0,1:T(8,128)(4,1)}, u32[]{:S(2)}) copy-start(pred[384,3072]{0,1:T(8,128)(4,1)} %broadcast_compare_fusion) | copy-start | bytes 3538948
Sparse Core Ops, SparseCore 0:
  10.2 323.8 all-gather.3
  350.1 80.9 all-gather.7
  432.8 70.5 all-gather.5
where the time goes:
time: 608 us; the launch traced here: 607 us
  waiting for transfers between devices  349 us (57%)
  matrix products  125 us (21%)
  other arithmetic  64 us (11%)
  local copies, waits for them, and re-layouts  43.7 us (7%)
  between operations  14.1 us (2%)
  starting transfers between devices  10 us (2%)
    all_gather x1, waiting for transfers between devices, shards(): segment = lax.all_gather(copies, ('dp', 'ctx'), axis=0, tiled=True)  299 us
    dot_general x1, matrix products, shards(): jnp.einsum('kgtn,nkd->tkgd', exp_terms.astype(jnp.bfloat16), value_split,...  56.9 us
    dot_general x1, matrix products, shards(): jnp.einsum('tkgd,nkd->kgtn', query_heads, key_split, preferred_element_ty...  56.4 us
    reduce_sum x1, other arithmetic, shards(): totals_next = jnp.sum(exp_terms, axis=3)  46.2 us
    all_gather x1, waiting for transfers between devices, shards(): key_block = lax.all_gather(key_rows, 'ctx', axis=0, tiled=True)  42.9 us
    unnamed x14, local copies, waits for them, and re-layouts  21.8 us
    dot_general x1, matrix products, shards(): jnp.dot(columns, segment, preferred_element_type=jnp.float32)  12.2 us
  transfers between devices with their start and end apart: 4, of which 3 were waited for; matrix products, arithmetic and copies ran while one was open for 25% of the time, Pallas kernels for 0%

commit v1 on v0

--- a/solution.py
+++ b/solution.py
@@ -132,8 +132,11 @@
     query_heads = queries[0].reshape(tok_rows, kv_heads, groups, head_dim)
     inv_root = 1.0 / math.sqrt(head_dim)
     best_score = jnp.full((kv_heads, groups, tok_rows), -1e30, jnp.float32)
-    key_block = lax.all_gather(key_rows, "ctx", axis=0, tiled=True)
-    value_block = lax.all_gather(value_rows, "ctx", axis=0, tiled=True)
+    key_block, value_block = jnp.split(
+        lax.all_gather(jnp.concatenate([key_rows, value_rows], axis=1), "ctx", axis=0, tiled=True),
+        [key_rows.shape[1]],
+        axis=1,
+    )
     block_rows = key_block.shape[0]
     key_pos = lookup(jnp.arange(block_rows, dtype=jnp.int32))
     key_split = key_block.reshape(block_rows, kv_heads, head_dim)

time: 608 us -> 674 us (1.11)
  waiting for transfers between devices: 349 us -> 409 us
    all_gather x2 -> x1, waiting for transfers between devices: 42.9 us -> 96.8 us  [shards(): lax.all_gather(jnp.concatenate([key_rows, value_rows], axis=1), 'ctx', ax...]
    unnamed x14 -> x13, local copies, waits for them, and re-layouts: 21.8 us -> 20.7 us
  transfers between devices with their start and end apart: 4 -> 3, of which waited for: 3 -> 3; matrix products, arithmetic and copies ran while one was open for 25% -> 7% of each run, Pallas kernels for 0% -> 0%
where the time goes in v1:
time: 674 us; the launch traced here: 672 us
  waiting for transfers between devices  409 us (61%)
  matrix products  125 us (19%)
  other arithmetic  65.7 us (10%)
  local copies, waits for them, and re-layouts  47.7 us (7%)
  between operations  14.3 us (2%)
  starting transfers between devices  9.99 us (1%)
    all_gather x1, waiting for transfers between devices, shards(): segment = lax.all_gather(copies, ('dp', 'ctx'), axis=0, tiled=True)  299 us
    all_gather x1, waiting for transfers between devices, shards(): lax.all_gather(jnp.concatenate([key_rows, value_rows], axis=1), 'ctx', ax...  96.8 us
    dot_general x1, matrix products, shards(): jnp.einsum('kgtn,nkd->tkgd', exp_terms.astype(jnp.bfloat16), value_split,...  57.1 us
    dot_general x1, matrix products, shards(): jnp.einsum('tkgd,nkd->kgtn', query_heads, key_split, preferred_element_ty...  55.6 us
    reduce_sum x1, other arithmetic, shards(): totals_next = jnp.sum(exp_terms, axis=3)  46.5 us
    unnamed x13, local copies, waits for them, and re-layouts  20.7 us
    all_to_all x1, waiting for transfers between devices, one_exchange(): tiles = lax.all_to_all(tiles, axis, split_axis=0, concat_axis=0, tiled=True)  13.6 us
  transfers between devices with their start and end apart: 3, of which 3 were waited for; matrix products, arithmetic and copies ran while one was open for 7% of the time, Pallas kernels for 0%

profile of v1, /device:TPU:4, one launch (start us, length us, event | category | flops | bytes accessed | tf_op | source)
XLA Modules:
  0.0 671.6 jit_solution(3340102781258294426)
XLA Ops:
  7.2 2.0 fusion.46
  9.3 0.8 copy.63
  10.2 0.7 compare_and_fusion.2
  10.9 0.1 broadcast_in_dim.87
  11.0 8.6 %copy.62 = bf16[1,384,8192]{1,2,0:T(8,128)(2,1)} copy(bf16[1,384,8192]{2,1,0:T(8,128)(2,1)} %param.11) | data formatting | bytes 12582912 | tf_op args[0]
  19.7 6.9 %gather_fusion = bf16[128,384,64]{1,2,0:T(8,128)(2,1)} fusion(bf16[384,128,64]{0,2,1:T(8,128)(2,1)} %bitcast.74, s32[1024]{0:T(1024)S(1)} %pad_clamp_fusion), kind=kCustom, calls=%fused_computation.2 | custom fusion | bytes 12583424 | tf_op jit(solution)/shard_map/jit(_take)/gather | solution.py:107
  26.6 0.1 select_reduce_fusion.1
  26.7 0.8 multiply_cosine_fusion
  27.5 8.0 %bitcast_select_fusion.1 = bf16[384,8192]{0,1:T(8,128)(2,1)} fusion(bf16[128,384,64]{1,2,0:T(8,128)(2,1)} %gather_fusion, pred[8192]{0:T(1024)(128)(4,1)S(1)} %broadcast_in_dim.87), kind=kLoop, calls=%fused_computation.11 | loop fusion | flops 3145728 | bytes 12591104 | tf_op jit(solution)/shard_map/jit(_take)/select_n | solution.py:107
  35.5 298.6 %all-gather.3.cloned.1.call-done = bf16[8192,1024]{1,0:T(8,128)(2,1)} async-done(((bf16[64,1024]{1,0:T(8,128)(2,1)}), bf16[8192,1024]{1,0:T(8,128)(2,1)}) %all-gather.3.cloned.1.call-update) | async-done | bytes 16777232 | tf_op jit(solution)/shard_map/all_gather | solution.py:110
  334.1 12.2 %fusion.50 = f32[384,1024]{1,0:T(8,128)S(1)} fusion(bf16[384,8192]{0,1:T(8,128)(2,1)} %bitcast_select_fusion.1, bf16[8192,1024]{1,0:T(8,128)(2,1)} %all-gather.3.cloned.1.call-done), kind=kOutput, calls=%fused_computation.97 | convolution fusion | flops 6442450944 | bytes 24641536 | tf_op jit(solution)/shard_map/dot_general | solution.py:112
  346.4 0.3 reshape.258
  346.7 0.6 subtract_convert_fusion
  347.4 0.5 pad_maximum_fusion.1
  348.0 1.0 pad_maximum_fusion
  349.0 0.2 copy.52
  349.2 0.2 copy.53
  349.4 0.2 copy.54
  349.6 0.1 maximum_bitcast_fusion
  349.7 0.8 gather_fusion.1
  350.6 0.2 select_bitcast_fusion.1
  350.8 1.9 reshape.305
  352.6 9.9 %all-to-all-start = ((f32[128,1,1536]{2,1,0:T(1,128)}), f32[128,1,1536]{2,1,0:T(1,128)S(1)}, u32[]{:S(2)}, u32[]{:S(2)}) async-start(f32[128,1,1536]{2,1,0:T(1,128)} %reshape.305), calls=%async_computation | async-start | bytes 1572864 | tf_op jit(solution)/shard_map/all_to_all | solution.py:38
  362.5 4.4 copy.76
  366.9 1.2 scatter_custom_fusion
  368.1 0.1 select_reduce_fusion
  368.3 2.2 broadcast_compare_fusion
  370.5 13.6 %all-to-all-done = f32[128,1,1536]{2,1,0:T(1,128)S(1)} async-done(((f32[128,1,1536]{2,1,0:T(1,128)}), f32[128,1,1536]{2,1,0:T(1,128)S(1)}, u32[]{:S(2)}, u32[]{:S(2)}) %all-to-all-start) | async-done | bytes 786464 | tf_op jit(solution)/shard_map/all_to_all | solution.py:38
  384.1 0.5 broadcast.364
  384.6 2.5 reduce
  387.1 0.3 reshape.306
  387.5 0.8 gather_fusion.2
  388.3 0.2 select_bitcast_fusion
  388.5 0.1 fusion.49
  388.6 0.1 copy.61
  388.7 0.9 squeeze.11
  389.6 0.1 copy.60
  389.7 0.9 squeeze.10
  390.6 0.1 copy.59
  390.7 0.9 squeeze.9
  391.6 96.8 %all-gather.5.cloned.1.call-done = bf16[3072,1024]{1,0:T(8,128)(2,1)} async-done(((bf16[384,1024]{1,0:T(8,128)(2,1)}), bf16[3072,1024]{1,0:T(8,128)(2,1)}) %all-gather.5.cloned.1.call-update) | async-done | bytes 6291472 | tf_op jit(solution)/shard_map/all_gather | solution.py:136
  488.4 4.9 fusion.48
  493.3 4.7 copy.72
  498.0 3.0 reshape.260
  500.9 55.6 %fusion = (f32[4,8,384]{2,1,0:T(8,128)S(1)}, f32[4,3072,384,8]{2,1,3,0:T(8,128)}) fusion(pred[384,3072]{0,1:T(8,128)(4,1)} %broadcast_compare_fusion, bf16[384,4,8,128]{3,2,1,0:T(8,128)(2,1)} %bitcast.77, bf16[3072,4,128,1]{2,1,0,3:T(4,128)(2,1)} %bitcast.80), kind=kOutput, calls=%fused_computation.6 | convolution fusion | flops 9776910336 | bytes 158515200 | tf_op jit(solution)/shard_map/tkgd,nkd->kgtn/dot_general | solution.py:144
  556.6 46.5 %fusion.1 = f32[4,8,384]{2,1,0:T(8,128)S(1)} fusion(f32[4,3072,384,8]{2,1,3,0:T(8,128)} %get-tuple-element.37, f32[4,8,384]{2,1,0:T(8,128)S(1)} %broadcast_maximum_fusion, pred[384,3072]{0,1:T(8,128)(4,1)S(1)} %copy-done), kind=kLoop, calls=%fused_computation.7 | loop fusion | flops 188731392 | bytes 152272896 | tf_op jit(solution)/shard_map/reduce_sum | solution.py:151
  603.1 57.1 %fusion.6 = bf16[384,4,8,128]{0,3,2,1:T(8,128)(2,1)} fusion(f32[384,4,8]{0,2,1:T(8,128)S(1)} %bitcast.86, bf16[3072,4,128,1]{0,2,3,1:T(8,128)(2,1)} %bitcast.78, f32[4,3072,384,8]{2,1,3,0:T(8,128)} %get-tuple-element.37, f32[4,8,384]{2,1,0:T(8,128)S(1)} %broadcast_maximum_fusion, pred[384,3072]{0,1:T(8,128)(4,1)S(1)} %copy-done), kind=kOutput, calls=%fused_computation.13 | convolution fusion | flops 9855565824 | bytes 158564352 | tf_op jit(solution)/shard_map/kgtn,nkd->tkgd/dot_general | solution.py:153
  660.1 4.6 copy.68
  (30 shorter events, 0.6 us)
Async XLA Ops:
  7.2 326.9 %all-gather.3.cloned.1.call-start = ((), (), s32[]{:S(2)}) async-start(), calls=%async_computation.1 | async-start | bytes 16908288 | tf_op jit(solution)/shard_map/all_gather | solution.py:110
  9.3 479.1 %all-gather.5.cloned.1.call-start = ((), (), s32[]{:S(2)}) async-start(), calls=%async_computation.2 | async-start | bytes 7077888 | tf_op jit(solution)/shard_map/all_gather | solution.py:136
  11.0 8.7 %copy-start.1 = (s32[128]{0:T(128)S(1)}, s32[128]{0:T(128)}, u32[]{:S(2)}) copy-start(s32[128]{0:T(128)} %param.17) | copy-start | bytes 1540
  347.3 2.3 copy-start.2
  352.6 31.5 %all-to-all-start = ((f32[128,1,1536]{2,1,0:T(1,128)}), f32[128,1,1536]{2,1,0:T(1,128)S(1)}, u32[]{:S(2)}, u32[]{:S(2)}) async-start(f32[128,1,1536]{2,1,0:T(1,128)} %reshape.305), calls=%async_computation | async-start | bytes 1572864 | tf_op jit(solution)/shard_map/all_to_all | solution.py:38
  500.9 55.7 %copy-start = (pred[384,3072]{0,1:T(8,128)(4,1)S(1)}, pred[384,3072]{0,1:T(8,128)(4,1)}, u32[]{:S(2)}) copy-start(pred[384,3072]{0,1:T(8,128)(4,1)} %broadcast_compare_fusion) | copy-start | bytes 3538948
Sparse Core Ops, SparseCore 0:
  10.2 323.8 all-gather.2
  349.1 139.2 all-gather.4
